TPU v7x, 256 devices: a whole 4x4x8 slice. The times are simulated.
256 devices in a mesh: line: 128 (over y, x, z_hi, core), view: 2 (over z_lo).
Axes of the slice: x: 4, y: 4, z: 8 (z_hi: 4, z_lo: 2; z = z_hi * 2 + z_lo), core: 2. Of those that a mesh axis runs over, the one named last changes fastest.
Arguments:
- light_field: bfloat16 [128, 8, 8, 8192], P('line', None, 'view'), may hold values from -6 to 6
- query_weight: bfloat16 [2, 64, 128], replicated, may hold values from -0.75 to 0.75
- key_weight: bfloat16 [2, 64, 128], replicated, may hold values from -24 to 24
- value_weight: bfloat16 [2, 64, 128], replicated, may hold values from -0.75 to 0.75
- out_weight: bfloat16 [2, 128, 64], replicated, may hold values from -0.5 to 0.5
- conv_first: bfloat16 [3, 3, 64, 64], replicated, may hold values from -0.25 to 0.25
- conv_second: bfloat16 [3, 3, 64, 64], replicated, may hold values from -0.25 to 0.25
Outputs:
- result: bfloat16 [128, 8, 8, 8192], P('line', None, 'view')
All inputs are finite; a program needn't handle non-finite values.
Results may differ from a plain program's by a relative error of at most 0.0069.
Values may be sent and summed in bfloat16 or wider, within the bound.
A program may use at most 64 MiB of HBM per device.

v0:
```python
import functools
import math

import jax
import jax.numpy as jnp
from jax import lax
from jax.experimental import pallas as pl
from jax.experimental.pallas import tpu as pltpu
from jax.sharding import PartitionSpec as P

F32 = jnp.float32
BF16 = jnp.bfloat16
MESH = pl.DeviceIdType.MESH

XY = 16
ZC = 16
VL = 4
CH = 64
WIDTH = 128
SCALE2 = math.log2(math.e) / math.sqrt(WIDTH)
GROUP = 32
TOK = 1024


def fold(n, body):
    def step(i, carry):
        body(i)
        return carry

    lax.fori_loop(0, n, step, 0)


def normalise(x, avg):
    mean = jnp.dot(x, avg[0:WIDTH, :], preferred_element_type=F32)
    centre = x.astype(F32) - mean
    square = centre * centre
    high = square.astype(BF16)
    low = (square - high.astype(F32)).astype(BF16)
    spread = jnp.dot(
        jnp.concatenate([high, low], axis=1), avg[...], preferred_element_type=F32
    )
    return (centre * lax.rsqrt(spread + 1e-05)).astype(BF16)


def attend_block(line, at, q_s, k_s, va_s, m_s):
    scores = lax.dot_general(
        q_s[line, at, :], k_s[line], (((1,), (1,)), ((), ())), preferred_element_type=F32
    )
    top = jnp.max(scores, axis=1, keepdims=True)
    e = jnp.exp2((scores - top) * SCALE2).astype(BF16)
    o = jnp.dot(e, va_s[line], preferred_element_type=F32)
    m_s[line, at, :] = (o[:, :WIDTH] / o[:, WIDTH:]).astype(BF16)


def kernel(
    x_ref, wq_ref, wk_ref, wv_ref, wo_ref, c1_ref, c2_ref, out_ref,
    w_qkv, w_out, w_c1, w_c2, avg, perm, perm_in, perm_out,
    q_s, k_s, va_s, m_s,
    y_send, a_recv, b_send, r_recv,
    tok, pad, hid,
    b2_send, a2_recv, y2_send, f_recv,
    s_a, r_a, s_b, r_b, s_h, r_h, s_g, r_g, s_b2, r_b2, s_a2, r_a2,
):
    line = lax.axis_index("line")
    view = lax.axis_index("view")
    xy = line // 8
    zc = line % 8
    me = zc * 2 + view
    core = zc % 2
    z = (zc // 2) * 2 + view
    far_xy = (xy + 15 + 2 * core) % 16
    far = far_xy * 8 + zc + 1 - 2 * core
    near = line + 1 - 2 * core

    def z_peer(t):
        return (xy * 8 + t // 2, t % 2)

    def xy_peer(t):
        return (t * 8 + zc, view)

    barrier = pltpu.get_barrier_semaphore()

    def greet(d):
        pl.semaphore_signal(barrier, inc=1, device_id=z_peer((me + d + 1) % 16), device_id_type=MESH)
        pl.semaphore_signal(barrier, inc=1, device_id=xy_peer((xy + d + 1) % 16), device_id_type=MESH)

    fold(15, greet)
    pl.semaphore_signal(barrier, inc=1, device_id=(far, view), device_id_type=MESH)

    w_qkv[...] = jnp.zeros_like(w_qkv)
    w_out[...] = jnp.zeros_like(w_out)
    for i in range(2):
        for n, ref in enumerate((wq_ref, wk_ref, wv_ref)):
            for h in range(2):
                w_qkv[i, h * CH : (h + 1) * CH, (2 * n + h) * WIDTH : (2 * n + h + 1) * WIDTH] = ref[i]
        none = jnp.zeros((WIDTH, CH), BF16)
        w_out[i, 0:WIDTH, :] = jnp.concatenate([wo_ref[i], none], axis=1)
        w_out[i, WIDTH:, :] = jnp.concatenate([none, wo_ref[i]], axis=1)
    row = lax.broadcasted_iota(jnp.int32, (WIDTH, WIDTH), 0)
    col = lax.broadcasted_iota(jnp.int32, (WIDTH, WIDTH), 1)
    same = jnp.where((row < CH) == (col < CH), 1.0 / CH, 0.0).astype(BF16)
    avg[0:WIDTH, :] = same
    avg[WIDTH:, :] = same
    row = lax.broadcasted_iota(jnp.int32, (256, 256), 0)
    col = lax.broadcasted_iota(jnp.int32, (256, 256), 1)
    perm[...] = jnp.where(
        jnp.logical_and(row // 16 == col % 16, row % 16 == col // 16), 1.0, 0.0
    ).astype(BF16)
    for ref, a, b in ((perm_in, row, col), (perm_out, col, row)):
        here = jnp.logical_and(a // 32 == (b // 2) % 8, (a // 2) % 16 == b // 16)
        ref[...] = jnp.where(jnp.logical_and(here, a % 2 == b % 2), 1.0, 0.0).astype(BF16)
    for ln in range(4):
        va_s[ln, :, WIDTH:] = jnp.ones((TOK, WIDTH), BF16)

    def project_to(i, pair, where):
        normed = normalise(pair, avg)
        rows = pair.shape[0]
        qkv = jnp.dot(normed, w_qkv[i], preferred_element_type=F32).astype(BF16)
        for h, (ln, start) in enumerate(where):
            at = pl.ds(start, rows)
            q_s[ln, at, :] = qkv[:, h * WIDTH : (h + 1) * WIDTH]
            k_s[ln, at, :] = qkv[:, (2 + h) * WIDTH : (3 + h) * WIDTH]
            va_s[ln, at, 0:WIDTH] = qkv[:, (4 + h) * WIDTH : (5 + h) * WIDTH]

    def horizontal(v):
        for p in range(2):
            project_to(
                0, x_ref[v, :, p * WIDTH : (p + 1) * WIDTH],
                [(0, 2 * p * 256), (0, (2 * p + 1) * 256)],
            )
        for b in range(4):
            attend_block(0, slice(b * 256, (b + 1) * 256), q_s, k_s, va_s, m_s)
        for p in range(2):
            lanes = slice(p * WIDTH, (p + 1) * WIDTH)
            mixed = jnp.concatenate(
                [m_s[0, 2 * p * 256 : (2 * p + 1) * 256, :], m_s[0, (2 * p + 1) * 256 : (2 * p + 2) * 256, :]],
                axis=1,
            )
            added = jnp.dot(mixed, w_out[0], preferred_element_type=F32)
            y_send[v, :, lanes] = (x_ref[v, :, lanes].astype(F32) + added).astype(BF16)

    def send_z(src, dst, v, s_sem, r_sem):
        pltpu.make_async_copy(src.at[v, pl.ds(me * 16, 16), :], dst.at[v, me], r_sem.at[v]).start()

        def one(d):
            j = d // 2
            there = (z + 8 + (4 - (j + 1) // 2) * (2 * (j % 2) - 1)) % 8
            t = (there // 2) * 4 + ((core + d + 1) % 2) * 2 + there % 2
            pltpu.make_async_remote_copy(
                src_ref=src.at[v, pl.ds(t * 16, 16), :], dst_ref=dst.at[v, me],
                send_sem=s_sem.at[v], recv_sem=r_sem.at[v],
                device_id=z_peer(t), device_id_type=MESH,
            ).start()

        fold(15, one)

    def send_xy(src, dst, v, s_sem, r_sem):
        pltpu.make_async_copy(src.at[v, pl.ds(xy * 16, 16), :], dst.at[v, xy], r_sem.at[v]).start()

        def one(d):
            t = (xy + d + 1) % 16
            pltpu.make_async_remote_copy(
                src_ref=src.at[v, pl.ds(t * 16, 16), :], dst_ref=dst.at[v, xy],
                send_sem=s_sem.at[v], recv_sem=r_sem.at[v],
                device_id=xy_peer(t), device_id_type=MESH,
            ).start()

        fold(15, one)

    def wait_all(ref, v, sem):
        pltpu.make_async_copy(ref.at[v], ref.at[v], sem.at[v]).wait()

    def wait_sent(ref, v, sem):
        part = ref.at[v, pl.ds(0, 15)]
        pltpu.make_async_copy(part, part, sem.at[v]).wait()

    def reorder(src, dst, v):
        rows = jnp.concatenate([src[v, s] for s in range(16)], axis=0)
        dst[v] = jnp.dot(perm[...], rows, preferred_element_type=F32).astype(BF16)

    def forward(v):
        wait_all(a_recv, v, r_a)
        reorder(a_recv, b_send, v)
        send_xy(b_send, r_recv, v, s_b, r_b)

    horizontal(0)
    pl.semaphore_wait(barrier, 31)
    send_z(y_send, a_recv, 0, s_a, r_a)

    horizontal(1)
    send_z(y_send, a_recv, 1, s_a, r_a)

    def rows_step(i):
        horizontal(i + 2)
        send_z(y_send, a_recv, i + 2, s_a, r_a)
        forward(i)

    fold(VL - 2, rows_step)

    w_c1[...] = jnp.zeros_like(w_c1)
    w_c2[...] = jnp.zeros_like(w_c2)
    none = jnp.zeros((CH, CH), BF16)
    for ref, dst, outs, shift in ((c1_ref, w_c1, 4, 0), (c2_ref, w_c2, 2, 1)):
        for dy in range(3):
            for d in (-1, 0, 1):
                if d == -1:
                    rows = [[none, none], [ref[dy, 0], none]]
                elif d == 0:
                    rows = [[ref[dy, 1], ref[dy, 0]], [ref[dy, 2], ref[dy, 1]]]
                else:
                    rows = [[none, ref[dy, 2]], [none, none]]
                tile = jnp.concatenate([jnp.concatenate(r, axis=1) for r in rows], axis=0)
                for po in range(outs):
                    pi = po + shift + d
                    if 0 <= pi < 4:
                        dst[
                            dy * 512 + pi * WIDTH : dy * 512 + (pi + 1) * WIDTH,
                            po * WIDTH : (po + 1) * WIDTH,
                        ] = tile

    def columns(v):
        wait_all(r_recv, v, r_b)
        rows = jnp.concatenate([r_recv[v, s] for s in range(16)], axis=0)
        tok[v] = jnp.dot(perm_in[...], rows, preferred_element_type=F32).astype(BF16)
        at = pl.multiple_of(v * 256, 256)
        for p in range(2):
            project_to(
                1, tok[v, :, p * WIDTH : (p + 1) * WIDTH], [(2 * p, at), (2 * p + 1, at)]
            )

    forward(2)
    fold(2, columns)
    forward(3)
    fold(2, lambda i: columns(i + 2))

    def attend_pair(p, v):
        at = pl.ds(pl.multiple_of(v * 256, 256), 256)
        for h in range(2):
            attend_block(2 * p + h, at, q_s, k_s, va_s, m_s)

    inner = slice(GROUP, GROUP + 256)

    def join(v):
        at = pl.ds(pl.multiple_of(v * 256, 256), 256)
        for p in range(2):
            mixed = jnp.concatenate([m_s[2 * p, at, :], m_s[2 * p + 1, at, :]], axis=1)
            added = jnp.dot(mixed, w_out[1], preferred_element_type=F32)
            x = tok[v, :, p * WIDTH : (p + 1) * WIDTH].astype(F32)
            pad[v, p + 1, inner, :] = (x + added).astype(BF16)

    left = jnp.where(core == 0, far, near)
    right = jnp.where(core == 0, near, far)

    def halos(v):
        return (
            pltpu.make_async_remote_copy(
                src_ref=pad.at[v, 1, inner, :], dst_ref=pad.at[v, 3, inner, :],
                send_sem=s_h.at[v], recv_sem=r_h.at[v],
                device_id=(left, view), device_id_type=MESH,
            ),
            pltpu.make_async_remote_copy(
                src_ref=pad.at[v, 2, inner, :], dst_ref=pad.at[v, 0, inner, :],
                send_sem=s_g.at[v], recv_sem=r_g.at[v],
                device_id=(right, view), device_id_type=MESH,
            ),
        )

    block = xy * 2 + core
    has_left = jnp.where(block == 0, 0.0, 1.0).astype(F32)
    has_right = jnp.where(block == 31, 0.0, 1.0).astype(F32)
    place = lax.broadcasted_iota(jnp.int32, (GROUP, WIDTH), 0)

    def rims(ref):
        for p in range(4):
            last = pltpu.roll(ref[p, 8 * GROUP : 9 * GROUP, :].astype(F32), 2, 0)
            ref[p, 0:GROUP, :] = jnp.where(place < 2, 0.0, last).astype(BF16)
            head = pltpu.roll(ref[p, GROUP : 2 * GROUP, :].astype(F32), GROUP - 2, 0)
            ref[p, 9 * GROUP :, :] = jnp.where(place >= GROUP - 2, 0.0, head).astype(BF16)

    def taps(ref):
        return jnp.concatenate(
            [ref[p, dy * GROUP : dy * GROUP + 256, :] for dy in range(3) for p in range(4)], axis=1
        )

    def convolve(v):
        for copy in halos(v):
            copy.wait()
        here = pad.at[v]
        here[0, inner, :] = (here[0, inner, :].astype(F32) * has_left).astype(BF16)
        here[3, inner, :] = (here[3, inner, :].astype(F32) * has_right).astype(BF16)
        rims(here)
        got = jnp.dot(taps(here), w_c1[...], preferred_element_type=F32)
        got = jnp.where(got >= 0, got, 0.1 * got)
        hid[0, inner, :] = (got[:, 0:WIDTH] * has_left).astype(BF16)
        hid[1, inner, :] = got[:, WIDTH : 2 * WIDTH].astype(BF16)
        hid[2, inner, :] = got[:, 2 * WIDTH : 3 * WIDTH].astype(BF16)
        hid[3, inner, :] = (got[:, 3 * WIDTH :] * has_right).astype(BF16)
        rims(hid)
        got = jnp.dot(taps(hid), w_c2[...], preferred_element_type=F32)
        second = jnp.concatenate([here[1, inner, :], here[2, inner, :]], axis=1)
        result = (second.astype(F32) + got).astype(BF16)
        b2_send[v] = jnp.dot(perm_out[...], result, preferred_element_type=F32).astype(BF16)
        send_xy(b2_send, a2_recv, v, s_b2, r_b2)

    def back(v):
        wait_all(a2_recv, v, r_b2)
        reorder(a2_recv, y2_send, v)
        send_z(y2_send, f_recv, v, s_a2, r_a2)

    def start_halos(v):
        attend_pair(1, v)
        join(v)
        for copy in halos(v):
            copy.start()

    attend_pair(0, 0)
    start_halos(0)
    attend_pair(0, 1)
    convolve(0)

    def columns_step(i):
        start_halos(i + 1)
        attend_pair(0, i + 2)
        convolve(i + 1)
        back(i)

    fold(2, columns_step)
    start_halos(3)
    convolve(3)
    back(2)
    back(3)

    def arrive(v):
        wait_all(f_recv, v, r_a2)
        out_ref[v] = f_recv[v]

    fold(VL, arrive)

    def drain(v):
        wait_sent(a_recv, v, s_a)
        wait_sent(r_recv, v, s_b)
        wait_sent(a2_recv, v, s_b2)
        wait_sent(f_recv, v, s_a2)

    fold(VL, drain)


def local(light_field, query_weight, key_weight, value_weight, out_weight, conv_first, conv_second):
    x = light_field.reshape(4, 2, VL, XY, 2, 256).transpose(2, 0, 4, 1, 3, 5)
    x = x.reshape(VL, 256, 256)
    vmem = pl.BlockSpec(memory_space=pltpu.VMEM)
    grid4 = pltpu.VMEM((VL, 16, 16, 256), BF16)
    flat4 = pltpu.VMEM((VL, 256, 256), BF16)
    sem = pltpu.SemaphoreType.DMA((VL,))
    got = pl.pallas_call(
        kernel,
        out_shape=jax.ShapeDtypeStruct((VL, 16, 16, 256), BF16),
        in_specs=[vmem] * 7,
        out_specs=vmem,
        scratch_shapes=[
            pltpu.VMEM((2, WIDTH, 6 * WIDTH), BF16),
            pltpu.VMEM((2, 2 * WIDTH, WIDTH), BF16),
            pltpu.VMEM((1536, 512), BF16),
            pltpu.VMEM((1536, 256), BF16),
            pltpu.VMEM((2 * WIDTH, WIDTH), BF16),
            pltpu.VMEM((256, 256), BF16),
            pltpu.VMEM((256, 256), BF16),
            pltpu.VMEM((256, 256), BF16),
            pltpu.VMEM((4, TOK, WIDTH), BF16),
            pltpu.VMEM((4, TOK, WIDTH), BF16),
            pltpu.VMEM((4, TOK, 2 * WIDTH), BF16),
            pltpu.VMEM((4, TOK, WIDTH), BF16),
            flat4, grid4, flat4, grid4,
            flat4,
            pltpu.VMEM((VL, 4, 10 * GROUP, WIDTH), BF16),
            pltpu.VMEM((4, 10 * GROUP, WIDTH), BF16),
            flat4, grid4, flat4, grid4,
            sem, sem, sem, sem, sem, sem, sem, sem, sem, sem, sem, sem,
        ],
        compiler_params=pltpu.CompilerParams(
            collective_id=0, has_side_effects=True, vmem_limit_bytes=48 << 20
        ),
    )(x, query_weight, key_weight, value_weight, out_weight, conv_first, conv_second)
    got = got.reshape(VL, 4, 2, 2, XY, 256).transpose(1, 3, 0, 4, 2, 5)
    return got.reshape(1, 8, VL, 8192)


def solution(mesh):
    placed = (P("line", None, "view", None), P(), P(), P(), P(), P(), P())
    return jax.shard_map(
        local, mesh=mesh, in_specs=placed, out_specs=P("line", None, "view", None), check_vma=False
    )
```

profile of v0, /device:TPU:1, one launch (start us, length us, event | category | flops | bytes accessed | tf_op | source)
XLA Modules:
  0.0 79.4 jit_solution(9745976327628050983)
XLA Ops:
  0.0 0.9 %copy.9.wo_ref = bf16[2,128,64]{2,1,0:T(8,128)(2,1)S(1)} copy(bf16[2,128,64]{1,2,0:T(8,128)(2,1)} %param.11) | data formatting | bytes 65536 | tf_op args[4]
  0.9 1.6 %reshape.12 = bf16[4,2,4,16,2,256]{5,4,3,2,1,0:T(2,128)(2,1)S(1)} reshape(bf16[1,8,4,8192]{3,2,1,0:T(4,128)(2,1)} %param.7) | data formatting | bytes 1048576 | tf_op jit(solution)/shard_map/reshape | solution.py:349
  2.5 0.0 copy-start
  2.5 0.0 copy-start.1
  2.5 0.0 copy-start.2
  2.5 0.0 copy-start.3
  2.5 0.0 copy-start.4
  2.5 0.1 copy.8
  2.6 0.8 copy-done
  3.4 0.1 copy-done.1
  3.5 0.0 copy-done.2
  3.5 0.0 copy-done.3
  3.5 0.0 copy-done.4
  3.5 74.2 %shard_map.73 = bf16[4,16,16,256]{3,2,1,0:T(8,128)(2,1)S(1)} custom-call(bf16[4,256,256]{2,1,0:T(8,128)(2,1)S(1)} %bitcast.6, bf16[2,64,128]{2,1,0:T(8,128)(2,1)S(1)} %copy-done.2, bf16[2,64,128]{2,1,0:T(8,128)(2,1)S(1)} %copy-done.3, bf16[2,64,128]{2,1,0:T(8,128)(2,1)S(1)} %copy-done.4, bf16[2,128,64]{2,1,0:T(8,128)(2,1)S(1)} %copy.9.wo_ref, ...), custom_call_target="tpu_custom_call" | custom-call | tf_op jit(solution)/shard_map/pallas_call | solution.py:355
  77.7 0.5 copy.10
  78.2 1.1 %reshape.15 = bf16[1,8,4,8192]{3,2,1,0:T(4,128)(2,1)} reshape(bf16[4,2,4,16,2,256]{5,4,3,2,1,0:T(2,128)(2,1)S(1)} %copy.10) | data formatting | bytes 1048576 | tf_op jit(solution)/shard_map/reshape | solution.py:385
Async XLA Ops:
  2.5 0.9 %copy-start = (bf16[3,3,64,64]{3,2,1,0:T(8,128)(2,1)S(1)}, bf16[3,3,64,64]{3,2,1,0:T(8,128)(2,1)}, u32[]{:S(2)}) copy-start(bf16[3,3,64,64]{3,2,1,0:T(8,128)(2,1)} %c1_ref.1) | copy-start | bytes 221188
  2.5 1.0 %copy-start.1 = (bf16[3,3,64,64]{3,2,1,0:T(8,128)(2,1)S(1)}, bf16[3,3,64,64]{3,2,1,0:T(8,128)(2,1)}, u32[]{:S(2)}) copy-start(bf16[3,3,64,64]{3,2,1,0:T(8,128)(2,1)} %c2_ref.1) | copy-start | bytes 221188
  2.5 1.0 %copy-start.2 = (bf16[2,64,128]{2,1,0:T(8,128)(2,1)S(1)}, bf16[2,64,128]{2,1,0:T(8,128)(2,1)}, u32[]{:S(2)}) copy-start(bf16[2,64,128]{2,1,0:T(8,128)(2,1)} %wq_ref.1) | copy-start | bytes 98308
  2.5 1.0 %copy-start.3 = (bf16[2,64,128]{2,1,0:T(8,128)(2,1)S(1)}, bf16[2,64,128]{2,1,0:T(8,128)(2,1)}, u32[]{:S(2)}) copy-start(bf16[2,64,128]{2,1,0:T(8,128)(2,1)} %wk_ref.1) | copy-start | bytes 98308
  2.5 0.9 %copy-start.4 = (bf16[2,64,128]{2,1,0:T(8,128)(2,1)S(1)}, bf16[2,64,128]{2,1,0:T(8,128)(2,1)}, u32[]{:S(2)}) copy-start(bf16[2,64,128]{2,1,0:T(8,128)(2,1)} %wv_ref.1) | copy-start | bytes 98308
where the time goes:
time: 79.6 us; the launch traced here: 79.4 us
  Pallas kernels  74.2 us (93%)
  local copies, waits for them, and re-layouts  5.07 us (6%)
    pallas_call x1, Pallas kernels, local(): pl.pallas_call(kernel, out_shape=jax.ShapeDtypeStruct((VL, 16, 16, 256),...  74.2 us
    unnamed x11, local copies, waits for them, and re-layouts  1.73 us
    reshape x2, local copies, waits for them, and re-layouts, local(): x = light_field.reshape(4, 2, VL, XY, 2, 256).transpose(2, 0, 4, 1, 3, 5)  1.67 us

commit v1 on v0

v1 whole, which is shorter than its diff:
```python
import functools
import math

import jax
import jax.numpy as jnp
from jax import lax
from jax.experimental import pallas as pl
from jax.experimental.pallas import tpu as pltpu
from jax.sharding import PartitionSpec as P

F32 = jnp.float32
BF16 = jnp.bfloat16
MESH = pl.DeviceIdType.MESH

XY = 16
ZC = 16
VL = 4
CH = 64
WIDTH = 128
SCALE2 = math.log2(math.e) / math.sqrt(WIDTH)
GROUP = 32
TOK = 1024


def snake(t):
    y = t // 4
    x = t % 4
    return 4 * y + x + (y % 2) * (3 - 2 * x)


def fold(n, body):
    def step(i, carry):
        body(i)
        return carry

    lax.fori_loop(0, n, step, 0)


def normalise(x, avg):
    mean = jnp.dot(x, avg[0:WIDTH, :], preferred_element_type=F32)
    centre = x.astype(F32) - mean
    square = centre * centre
    high = square.astype(BF16)
    low = (square - high.astype(F32)).astype(BF16)
    spread = jnp.dot(
        jnp.concatenate([high, low], axis=1), avg[...], preferred_element_type=F32
    )
    return (centre * lax.rsqrt(spread + 1e-05)).astype(BF16)


def attend_block(line, at, q_s, k_s, va_s, m_s):
    scores = lax.dot_general(
        q_s[line, at, :], k_s[line], (((1,), (1,)), ((), ())), preferred_element_type=F32
    )
    top = jnp.max(scores, axis=1, keepdims=True)
    e = jnp.exp2((scores - top) * SCALE2).astype(BF16)
    o = jnp.dot(e, va_s[line], preferred_element_type=F32)
    m_s[line, at, :] = (o[:, :WIDTH] / o[:, WIDTH:]).astype(BF16)


def kernel(
    x_hbm, wq_hbm, wk_hbm, wv_hbm, wo_hbm, c1_hbm, c2_hbm, out_ref,
    x_in, wq_ref, wk_ref, wv_ref, wo_ref, c1_ref, c2_ref, x_rows,
    w_qkv, w_out, w_c1, w_c2, avg, perm, perm_in, perm_out, perm_end,
    q_s, k_s, va_s, m_s,
    y_send, a_recv, b_send, r_recv,
    tok, pad, hid,
    b2_send, a2_recv, y2_send, f_recv,
    l_sem, s_a, r_a, s_b, r_b, s_h, r_h, s_g, r_g, s_b2, r_b2, s_a2, r_a2,
):
    line = lax.axis_index("line")
    view = lax.axis_index("view")
    xy = line // 8
    zc = line % 8
    me = zc * 2 + view
    core = zc % 2
    z = (zc // 2) * 2 + view
    place_xy = snake(xy)
    far_xy = snake((place_xy + 15 + 2 * core) % 16)
    far = far_xy * 8 + zc + 1 - 2 * core
    near = line + 1 - 2 * core

    def z_peer(t):
        return (xy * 8 + t // 2, t % 2)

    def xy_peer(t):
        return (t * 8 + zc, view)

    barrier = pltpu.get_barrier_semaphore()

    def greet(d):
        pl.semaphore_signal(barrier, inc=1, device_id=z_peer((me + d + 1) % 16), device_id_type=MESH)
        pl.semaphore_signal(barrier, inc=1, device_id=xy_peer((xy + d + 1) % 16), device_id_type=MESH)

    fold(15, greet)
    pl.semaphore_signal(barrier, inc=1, device_id=(far, view), device_id_type=MESH)

    loads = [
        pltpu.make_async_copy(src, dst, l_sem.at[i])
        for i, (src, dst) in enumerate(
            (
                (x_hbm, x_in), (wq_hbm, wq_ref), (wk_hbm, wk_ref), (wv_hbm, wv_ref),
                (wo_hbm, wo_ref), (c1_hbm, c1_ref), (c2_hbm, c2_ref),
            )
        )
    ]
    for load in loads:
        load.start()
    for load in loads:
        load.wait()

    w_qkv[...] = jnp.zeros_like(w_qkv)
    w_out[...] = jnp.zeros_like(w_out)
    for i in range(2):
        for n, ref in enumerate((wq_ref, wk_ref, wv_ref)):
            for h in range(2):
                w_qkv[i, h * CH : (h + 1) * CH, (2 * n + h) * WIDTH : (2 * n + h + 1) * WIDTH] = ref[i]
        w_out[i, 0:CH, 0:WIDTH] = wo_ref[i]
        w_out[i, CH:, WIDTH:] = wo_ref[i]
    row = lax.broadcasted_iota(jnp.int32, (WIDTH, WIDTH), 0)
    col = lax.broadcasted_iota(jnp.int32, (WIDTH, WIDTH), 1)
    same = jnp.where((row < CH) == (col < CH), 1.0 / CH, 0.0).astype(BF16)
    avg[0:WIDTH, :] = same
    avg[WIDTH:, :] = same
    row = lax.broadcasted_iota(jnp.int32, (256, 256), 0)
    col = lax.broadcasted_iota(jnp.int32, (256, 256), 1)
    perm[...] = jnp.where(
        jnp.logical_and(row // 16 == col % 16, row % 16 == col // 16), 1.0, 0.0
    ).astype(BF16)
    for ref, a, b in ((perm_in, row, col), (perm_out, col, row)):
        for odd in range(2):
            if odd:
                here = jnp.logical_and(a // 32 == b // 32, (a // 2) % 16 == b % 16)
                here = jnp.logical_and(here, a % 2 == (b // 16) % 2)
            else:
                here = jnp.logical_and(a // 32 == (b // 2) % 8, (a // 2) % 16 == b // 16)
                here = jnp.logical_and(here, a % 2 == b % 2)
            ref[odd] = jnp.where(here, 1.0, 0.0).astype(BF16)
    chip = snake(row % 16)
    for odd in range(2):
        if odd:
            here = jnp.logical_and(col % 16 == chip, col // 16 == row // 16)
        else:
            here = jnp.logical_and(col // 16 == chip, col % 16 == row // 16)
        perm_end[odd] = jnp.where(here, 1.0, 0.0).astype(BF16)
    for ln in range(4):
        va_s[ln, :, WIDTH:] = jnp.ones((TOK, WIDTH), BF16)

    w_c1[...] = jnp.zeros_like(w_c1)
    w_c2[...] = jnp.zeros_like(w_c2)
    none = jnp.zeros((CH, CH), BF16)
    for ref, dst, outs, shift in ((c1_ref, w_c1, 4, 0), (c2_ref, w_c2, 2, 1)):
        for dy in range(3):
            for d in (-1, 0, 1):
                if d == -1:
                    rows = [[none, none], [ref[dy, 0], none]]
                elif d == 0:
                    rows = [[ref[dy, 1], ref[dy, 0]], [ref[dy, 2], ref[dy, 1]]]
                else:
                    rows = [[none, ref[dy, 2]], [none, none]]
                tile = jnp.concatenate([jnp.concatenate(r, axis=1) for r in rows], axis=0)
                for po in range(outs):
                    pi = po + shift + d
                    if 0 <= pi < 4:
                        dst[
                            dy * 512 + pi * WIDTH : dy * 512 + (pi + 1) * WIDTH,
                            po * WIDTH : (po + 1) * WIDTH,
                        ] = tile

    def bring(t):
        for d in range(16):
            start = pl.multiple_of(snake(t) * 512 + (d // 2) % 2 * 256, 256)
            rays = x_in[(d // 4) * 2 + d % 2, :, pl.ds(start, 256)].astype(F32)
            for p in range(2):
                x_rows[p, pl.ds(d * 16 + t, VL, stride=256), :] = rays[:, p * WIDTH : (p + 1) * WIDTH]

    fold(16, bring)

    def project_to(i, pair, where):
        normed = normalise(pair, avg)
        rows = pair.shape[0]
        qkv = jnp.dot(normed, w_qkv[i], preferred_element_type=F32).astype(BF16)
        for h, (ln, start) in enumerate(where):
            at = pl.ds(start, rows)
            q_s[ln, at, :] = qkv[:, h * WIDTH : (h + 1) * WIDTH]
            k_s[ln, at, :] = qkv[:, (2 + h) * WIDTH : (3 + h) * WIDTH]
            va_s[ln, at, 0:WIDTH] = qkv[:, (4 + h) * WIDTH : (5 + h) * WIDTH]

    def out_project(i, mixed):
        return lax.dot_general(
            mixed, w_out[i], (((1,), (1,)), ((), ())), preferred_element_type=F32
        )

    def horizontal(v):
        at = pl.ds(pl.multiple_of(v * 256, 256), 256)
        for p in range(2):
            project_to(
                0, x_rows[p, at, :].astype(BF16), [(0, 2 * p * 256), (0, (2 * p + 1) * 256)]
            )
        for b in range(4):
            attend_block(0, slice(b * 256, (b + 1) * 256), q_s, k_s, va_s, m_s)
        for p in range(2):
            mixed = jnp.concatenate(
                [m_s[0, 2 * p * 256 : (2 * p + 1) * 256, :], m_s[0, (2 * p + 1) * 256 : (2 * p + 2) * 256, :]],
                axis=1,
            )
            added = out_project(0, mixed)
            y_send[v, :, p * WIDTH : (p + 1) * WIDTH] = (x_rows[p, at, :] + added).astype(BF16)

        @pl.when(v % 2 == 1)
        def _():
            y_send[v] = jnp.dot(perm[...], y_send[v], preferred_element_type=F32).astype(BF16)

    def send_z(src, dst, v, s_sem, r_sem):
        pltpu.make_async_copy(src.at[v, pl.ds(me * 16, 16), :], dst.at[v, me], r_sem.at[v]).start()

        def one(d):
            j = d // 2
            there = (z + 8 + (4 - (j + 1) // 2) * (2 * (j % 2) - 1)) % 8
            t = (there // 2) * 4 + ((core + d + 1) % 2) * 2 + there % 2
            pltpu.make_async_remote_copy(
                src_ref=src.at[v, pl.ds(t * 16, 16), :], dst_ref=dst.at[v, me],
                send_sem=s_sem.at[v], recv_sem=r_sem.at[v],
                device_id=z_peer(t), device_id_type=MESH,
            ).start()

        fold(15, one)

    def send_xy(src, dst, v, s_sem, r_sem):
        pltpu.make_async_copy(src.at[v, pl.ds(xy * 16, 16), :], dst.at[v, xy], r_sem.at[v]).start()

        def one(d):
            t = (xy + d + 1) % 16
            pltpu.make_async_remote_copy(
                src_ref=src.at[v, pl.ds(t * 16, 16), :], dst_ref=dst.at[v, xy],
                send_sem=s_sem.at[v], recv_sem=r_sem.at[v],
                device_id=xy_peer(t), device_id_type=MESH,
            ).start()

        fold(15, one)

    def wait_all(ref, v, sem):
        pltpu.make_async_copy(ref.at[v], ref.at[v], sem.at[v]).wait()

    def wait_sent(ref, v, sem):
        part = ref.at[v, pl.ds(0, 15)]
        pltpu.make_async_copy(part, part, sem.at[v]).wait()

    def reorder(src, dst, v):
        rows = jnp.concatenate([src[v, s] for s in range(16)], axis=0)
        dst[v] = jnp.dot(perm[...], rows, preferred_element_type=F32).astype(BF16)

    def first_stage(along_z, src, dst, v, s_sem, r_sem):
        @pl.when(along_z)
        def _():
            send_z(src, dst, v, s_sem, r_sem)

        @pl.when(jnp.logical_not(along_z))
        def _():
            send_xy(src, dst, v, s_sem, r_sem)

    def start(v):
        first_stage(v % 2 == 0, y_send, a_recv, v, s_a, r_a)

    def forward(v):
        wait_all(a_recv, v, r_a)
        reorder(a_recv, b_send, v)
        first_stage(v % 2 == 1, b_send, r_recv, v, s_b, r_b)

    def rows_step(v):
        horizontal(v)

        @pl.when(v == 1)
        def _():
            pl.semaphore_wait(barrier, 31)
            start(0)

        @pl.when(v > 0)
        def _():
            start(v)

    fold(VL, rows_step)
    fold(VL, lambda i: forward(i + 1 - 2 * (i % 2)))

    def columns(v):
        wait_all(r_recv, v, r_b)
        rows = jnp.concatenate([r_recv[v, s] for s in range(16)], axis=0)
        tok[v] = jnp.dot(perm_in[v % 2], rows, preferred_element_type=F32).astype(BF16)
        at = pl.multiple_of(v * 256, 256)
        for p in range(2):
            project_to(
                1, tok[v, :, p * WIDTH : (p + 1) * WIDTH], [(2 * p, at), (2 * p + 1, at)]
            )

    fold(VL, columns)

    inner = slice(GROUP, GROUP + 256)

    def attend(v):
        at = pl.ds(pl.multiple_of(v * 256, 256), 256)
        for ln in range(4):
            attend_block(ln, at, q_s, k_s, va_s, m_s)
        for p in range(2):
            mixed = jnp.concatenate([m_s[2 * p, at, :], m_s[2 * p + 1, at, :]], axis=1)
            added = out_project(1, mixed)
            x = tok[v, :, p * WIDTH : (p + 1) * WIDTH].astype(F32)
            pad[v, p + 1, inner, :] = (x + added).astype(BF16)
        for copy in halos(v):
            copy.start()

    left = jnp.where(core == 0, far, near)
    right = jnp.where(core == 0, near, far)

    def halos(v):
        return (
            pltpu.make_async_remote_copy(
                src_ref=pad.at[v, 1, inner, :], dst_ref=pad.at[v, 3, inner, :],
                send_sem=s_h.at[v], recv_sem=r_h.at[v],
                device_id=(left, view), device_id_type=MESH,
            ),
            pltpu.make_async_remote_copy(
                src_ref=pad.at[v, 2, inner, :], dst_ref=pad.at[v, 0, inner, :],
                send_sem=s_g.at[v], recv_sem=r_g.at[v],
                device_id=(right, view), device_id_type=MESH,
            ),
        )

    block = place_xy * 2 + core
    has_left = jnp.where(block == 0, 0.0, 1.0).astype(F32)
    has_right = jnp.where(block == 31, 0.0, 1.0).astype(F32)
    place = lax.broadcasted_iota(jnp.int32, (GROUP, WIDTH), 0)

    def rims(ref):
        for p in range(4):
            last = pltpu.roll(ref[p, 8 * GROUP : 9 * GROUP, :].astype(F32), 2, 0)
            ref[p, 0:GROUP, :] = jnp.where(place < 2, 0.0, last).astype(BF16)
            head = pltpu.roll(ref[p, GROUP : 2 * GROUP, :].astype(F32), GROUP - 2, 0)
            ref[p, 9 * GROUP :, :] = jnp.where(place >= GROUP - 2, 0.0, head).astype(BF16)

    def taps(ref):
        return jnp.concatenate(
            [ref[p, dy * GROUP : dy * GROUP + 256, :] for dy in range(3) for p in range(4)], axis=1
        )

    def convolve(v):
        for copy in halos(v):
            copy.wait()
        here = pad.at[v]
        here[0, inner, :] = (here[0, inner, :].astype(F32) * has_left).astype(BF16)
        here[3, inner, :] = (here[3, inner, :].astype(F32) * has_right).astype(BF16)
        rims(here)
        got = jnp.dot(taps(here), w_c1[...], preferred_element_type=F32)
        got = jnp.where(got >= 0, got, 0.1 * got)
        hid[0, inner, :] = (got[:, 0:WIDTH] * has_left).astype(BF16)
        hid[1, inner, :] = got[:, WIDTH : 2 * WIDTH].astype(BF16)
        hid[2, inner, :] = got[:, 2 * WIDTH : 3 * WIDTH].astype(BF16)
        hid[3, inner, :] = (got[:, 3 * WIDTH :] * has_right).astype(BF16)
        rims(hid)
        got = jnp.dot(taps(hid), w_c2[...], preferred_element_type=F32)
        second = jnp.concatenate([here[1, inner, :], here[2, inner, :]], axis=1)
        result = (second.astype(F32) + got).astype(BF16)
        late = v // 3
        b2_send[v] = jnp.dot(perm_out[1 - late], result, preferred_element_type=F32).astype(BF16)
        first_stage(v < 3, b2_send, a2_recv, v, s_b2, r_b2)

    def back(v):
        wait_all(a2_recv, v, r_b2)
        reorder(a2_recv, y2_send, v)
        first_stage(v == 3, y2_send, f_recv, v, s_a2, r_a2)

    def columns_step(i):
        @pl.when(i < VL)
        def _():
            attend(i)

        @pl.when(i > 0)
        def _():
            convolve(i - 1)

    fold(VL + 1, columns_step)
    fold(VL, lambda i: back(i + i // 2 - 3 * (i // 3) + i // 3))

    def arrive(v):
        wait_all(f_recv, v, r_a2)
        rows = jnp.concatenate([f_recv[v, s] for s in range(16)], axis=0)
        got = jnp.dot(perm_end[v // 3], rows, preferred_element_type=F32).astype(BF16)
        for s in range(16):
            out_ref[v, s] = got[s * 16 : (s + 1) * 16, :]

    fold(VL, arrive)

    def drain(v):
        wait_sent(a_recv, v, s_a)
        wait_sent(r_recv, v, s_b)
        wait_sent(a2_recv, v, s_b2)
        wait_sent(f_recv, v, s_a2)

    fold(VL, drain)


def local(light_field, query_weight, key_weight, value_weight, out_weight, conv_first, conv_second):
    x = light_field.reshape(8, VL, 8192)
    vmem = pl.BlockSpec(memory_space=pltpu.VMEM)
    grid4 = pltpu.VMEM((VL, 16, 16, 256), BF16)
    flat4 = pltpu.VMEM((VL, 256, 256), BF16)
    sem = pltpu.SemaphoreType.DMA((VL,))
    weight = pltpu.VMEM((2, CH, WIDTH), BF16)
    taps = pltpu.VMEM((3, 3, CH, CH), BF16)
    got = pl.pallas_call(
        kernel,
        out_shape=jax.ShapeDtypeStruct((VL, 16, 16, 256), BF16),
        in_specs=[pl.BlockSpec(memory_space=pltpu.MemorySpace.HBM)] * 7,
        out_specs=vmem,
        scratch_shapes=[
            pltpu.VMEM((8, VL, 8192), BF16),
            weight, weight, weight, weight, taps, taps,
            pltpu.VMEM((2, TOK, WIDTH), F32),
            pltpu.VMEM((2, WIDTH, 6 * WIDTH), BF16),
            pltpu.VMEM((2, WIDTH, 2 * WIDTH), BF16),
            pltpu.VMEM((1536, 512), BF16),
            pltpu.VMEM((1536, 256), BF16),
            pltpu.VMEM((2 * WIDTH, WIDTH), BF16),
            pltpu.VMEM((256, 256), BF16),
            pltpu.VMEM((2, 256, 256), BF16),
            pltpu.VMEM((2, 256, 256), BF16),
            pltpu.VMEM((2, 256, 256), BF16),
            pltpu.VMEM((4, TOK, WIDTH), BF16),
            pltpu.VMEM((4, TOK, WIDTH), BF16),
            pltpu.VMEM((4, TOK, 2 * WIDTH), BF16),
            pltpu.VMEM((4, TOK, WIDTH), BF16),
            flat4, grid4, flat4, grid4,
            flat4,
            pltpu.VMEM((VL, 4, 10 * GROUP, WIDTH), BF16),
            pltpu.VMEM((4, 10 * GROUP, WIDTH), BF16),
            flat4, grid4, flat4, grid4,
            pltpu.SemaphoreType.DMA((7,)),
            sem, sem, sem, sem, sem, sem, sem, sem, sem, sem, sem, sem,
        ],
        compiler_params=pltpu.CompilerParams(
            collective_id=0, has_side_effects=True, vmem_limit_bytes=48 << 20
        ),
    )(x, query_weight, key_weight, value_weight, out_weight.transpose(0, 2, 1), conv_first, conv_second)
    got = got.reshape(VL, 4, 2, 2, XY, 256).transpose(1, 3, 0, 4, 2, 5)
    return got.reshape(1, 8, VL, 8192)


def solution(mesh):
    placed = (P("line", None, "view", None), P(), P(), P(), P(), P(), P())
    return jax.shard_map(
        local, mesh=mesh, in_specs=placed, out_specs=P("line", None, "view", None), check_vma=False
    )
```

time: 79.6 us -> 71.9 us (0.903)
  Pallas kernels: 74.2 us -> 63.9 us
  local copies, waits for them, and re-layouts: 5.07 us -> 7.56 us
    pallas_call x1, Pallas kernels: 74.2 us -> 63.9 us  [local(): pl.pallas_call(kernel, out_shape=jax.ShapeDtypeStruct((VL, 16, 16, 256),...]
    unnamed x11 -> x14, local copies, waits for them, and re-layouts: 1.73 us -> 5.89 us
    reshape x2 -> x0, local copies, waits for them, and re-layouts: 1.67 us -> none  [local(): x = light_field.reshape(4, 2, VL, XY, 2, 256).transpose(2, 0, 4, 1, 3, 5)]
where the time goes in v1:
time: 71.9 us; the launch traced here: 71.5 us
  Pallas kernels  63.9 us (89%)
  local copies, waits for them, and re-layouts  7.56 us (11%)
    pallas_call x1, Pallas kernels, local(): pl.pallas_call(kernel, out_shape=jax.ShapeDtypeStruct((VL, 16, 16, 256),...  63.9 us
    unnamed x14, local copies, waits for them, and re-layouts  5.89 us

profile of v1, /device:TPU:1, one launch (start us, length us, event | category | flops | bytes accessed | tf_op | source)
XLA Modules:
  0.0 71.5 jit_solution(6402811129972933094)
XLA Ops:
  0.0 0.0 copy-start
  0.0 1.0 %copy-done = bf16[1,8,4,8192]{3,2,1,0:T(4,128)(2,1)S(1)} copy-done((bf16[1,8,4,8192]{3,2,1,0:T(4,128)(2,1)S(1)}, bf16[1,8,4,8192]{3,2,1,0:T(4,128)(2,1)}, u32[]{:S(2)}) %copy-start) | copy-done | bytes 524312
  1.0 0.0 copy-start.1
  1.0 0.9 %copy-done.1 = bf16[3,3,64,64]{3,2,1,0:T(8,128)(2,1)S(1)} copy-done((bf16[3,3,64,64]{3,2,1,0:T(8,128)(2,1)S(1)}, bf16[3,3,64,64]{3,2,1,0:T(8,128)(2,1)}, u32[]{:S(2)}) %copy-start.1) | copy-done | bytes 73752
  2.0 0.0 copy-start.2
  2.0 0.9 %copy-done.2 = bf16[3,3,64,64]{3,2,1,0:T(8,128)(2,1)S(1)} copy-done((bf16[3,3,64,64]{3,2,1,0:T(8,128)(2,1)S(1)}, bf16[3,3,64,64]{3,2,1,0:T(8,128)(2,1)}, u32[]{:S(2)}) %copy-start.2) | copy-done | bytes 73752
  2.9 0.0 copy-start.3
  2.9 0.8 %copy-done.3 = bf16[2,64,128]{2,1,0:T(8,128)(2,1)S(1)} copy-done((bf16[2,64,128]{2,1,0:T(8,128)(2,1)S(1)}, bf16[2,64,128]{2,1,0:T(8,128)(2,1)}, u32[]{:S(2)}) %copy-start.3) | copy-done | bytes 32792
  3.6 0.0 copy-start.4
  3.6 0.8 %copy-done.4 = bf16[2,64,128]{2,1,0:T(8,128)(2,1)S(1)} copy-done((bf16[2,64,128]{2,1,0:T(8,128)(2,1)S(1)}, bf16[2,64,128]{2,1,0:T(8,128)(2,1)}, u32[]{:S(2)}) %copy-start.4) | copy-done | bytes 32792
  4.4 0.0 copy-start.5
  4.4 0.8 %copy-done.5 = bf16[2,64,128]{2,1,0:T(8,128)(2,1)S(1)} copy-done((bf16[2,64,128]{2,1,0:T(8,128)(2,1)S(1)}, bf16[2,64,128]{2,1,0:T(8,128)(2,1)}, u32[]{:S(2)}) %copy-start.5) | copy-done | bytes 32792
  5.1 0.0 copy-start.6
  5.1 0.8 %copy-done.6 = bf16[2,128,64]{1,2,0:T(8,128)(2,1)S(1)} copy-done((bf16[2,128,64]{1,2,0:T(8,128)(2,1)S(1)}, bf16[2,128,64]{1,2,0:T(8,128)(2,1)}, u32[]{:S(2)}) %copy-start.6) | copy-done | bytes 32792
  5.9 63.9 %shard_map.73 = bf16[4,16,16,256]{3,2,1,0:T(8,128)(2,1)S(1)} custom-call(bf16[8,4,8192]{2,1,0:T(4,128)(2,1)S(1)} %bitcast.6, bf16[2,64,128]{2,1,0:T(8,128)(2,1)S(1)} %copy-done.3, bf16[2,64,128]{2,1,0:T(8,128)(2,1)S(1)} %copy-done.4, bf16[2,64,128]{2,1,0:T(8,128)(2,1)S(1)} %copy-done.5, bf16[2,64,128]{2,1,0:T(8,128)(2,1)S(1)} %bitcast.7, ...), custom_call_target="tpu_custom_call" | custom-call | tf_op jit(solution)/shard_map/pallas_call | solution.py:409
  69.8 0.5 copy.8
  70.4 1.1 %reshape.11 = bf16[1,8,4,8192]{3,2,1,0:T(4,128)(2,1)} reshape(bf16[4,2,4,16,2,256]{5,4,3,2,1,0:T(2,128)(2,1)S(1)} %copy.8) | data formatting | bytes 1048576 | tf_op jit(solution)/shard_map/reshape | solution.py:444
Async XLA Ops:
  0.0 1.0 %copy-start = (bf16[1,8,4,8192]{3,2,1,0:T(4,128)(2,1)S(1)}, bf16[1,8,4,8192]{3,2,1,0:T(4,128)(2,1)}, u32[]{:S(2)}) copy-start(bf16[1,8,4,8192]{3,2,1,0:T(4,128)(2,1)} %param.7) | copy-start | bytes 1572868
  1.0 0.9 %copy-start.1 = (bf16[3,3,64,64]{3,2,1,0:T(8,128)(2,1)S(1)}, bf16[3,3,64,64]{3,2,1,0:T(8,128)(2,1)}, u32[]{:S(2)}) copy-start(bf16[3,3,64,64]{3,2,1,0:T(8,128)(2,1)} %c1_hbm.1) | copy-start | bytes 221188
  2.0 0.9 %copy-start.2 = (bf16[3,3,64,64]{3,2,1,0:T(8,128)(2,1)S(1)}, bf16[3,3,64,64]{3,2,1,0:T(8,128)(2,1)}, u32[]{:S(2)}) copy-start(bf16[3,3,64,64]{3,2,1,0:T(8,128)(2,1)} %c2_hbm.1) | copy-start | bytes 221188
  2.9 0.8 %copy-start.3 = (bf16[2,64,128]{2,1,0:T(8,128)(2,1)S(1)}, bf16[2,64,128]{2,1,0:T(8,128)(2,1)}, u32[]{:S(2)}) copy-start(bf16[2,64,128]{2,1,0:T(8,128)(2,1)} %wq_hbm.1) | copy-start | bytes 98308
  3.6 0.8 %copy-start.4 = (bf16[2,64,128]{2,1,0:T(8,128)(2,1)S(1)}, bf16[2,64,128]{2,1,0:T(8,128)(2,1)}, u32[]{:S(2)}) copy-start(bf16[2,64,128]{2,1,0:T(8,128)(2,1)} %wk_hbm.1) | copy-start | bytes 98308
  4.4 0.8 %copy-start.5 = (bf16[2,64,128]{2,1,0:T(8,128)(2,1)S(1)}, bf16[2,64,128]{2,1,0:T(8,128)(2,1)}, u32[]{:S(2)}) copy-start(bf16[2,64,128]{2,1,0:T(8,128)(2,1)} %wv_hbm.1) | copy-start | bytes 98308
  5.1 0.8 %copy-start.6 = (bf16[2,128,64]{1,2,0:T(8,128)(2,1)S(1)}, bf16[2,128,64]{1,2,0:T(8,128)(2,1)}, u32[]{:S(2)}) copy-start(bf16[2,128,64]{1,2,0:T(8,128)(2,1)} %param.11) | copy-start | bytes 98308

commit v2 on v1

--- a/solution.py
+++ b/solution.py
@@ -61,7 +61,7 @@
 def kernel(
     x_hbm, wq_hbm, wk_hbm, wv_hbm, wo_hbm, c1_hbm, c2_hbm, out_ref,
     x_in, wq_ref, wk_ref, wv_ref, wo_ref, c1_ref, c2_ref, x_rows,
-    w_qkv, w_out, w_c1, w_c2, avg, perm, perm_in, perm_out, perm_end,
+    w_qkv, w_out, w_c1, w_c1b, w_c2, avg, perm, perm_in, perm_out, perm_end,
     q_s, k_s, va_s, m_s,
     y_send, a_recv, b_send, r_recv,
     tok, pad, hid,
@@ -86,11 +86,22 @@
     def xy_peer(t):
         return (t * 8 + zc, view)
 
+    def z_order(d):
+        j = d // 2
+        there = (z + 8 + (4 - (j + 1) // 2) * (2 * (j % 2) - 1)) % 8
+        return (there // 2) * 4 + ((core + d + 1) % 2) * 2 + there % 2
+
+    def hop(j):
+        return (2 - j + (j // 2) * (2 * j - 1)) % 4
+
+    def xy_order(d):
+        return ((xy // 4 + hop(d // 4)) % 4) * 4 + (xy % 4 + hop(d % 4)) % 4
+
     barrier = pltpu.get_barrier_semaphore()
 
     def greet(d):
-        pl.semaphore_signal(barrier, inc=1, device_id=z_peer((me + d + 1) % 16), device_id_type=MESH)
-        pl.semaphore_signal(barrier, inc=1, device_id=xy_peer((xy + d + 1) % 16), device_id_type=MESH)
+        pl.semaphore_signal(barrier, inc=1, device_id=z_peer(z_order(d)), device_id_type=MESH)
+        pl.semaphore_signal(barrier, inc=1, device_id=xy_peer(xy_order(d)), device_id_type=MESH)
 
     fold(15, greet)
     pl.semaphore_signal(barrier, inc=1, device_id=(far, view), device_id_type=MESH)
@@ -146,26 +157,18 @@
     for ln in range(4):
         va_s[ln, :, WIDTH:] = jnp.ones((TOK, WIDTH), BF16)
 
-    w_c1[...] = jnp.zeros_like(w_c1)
-    w_c2[...] = jnp.zeros_like(w_c2)
     none = jnp.zeros((CH, CH), BF16)
-    for ref, dst, outs, shift in ((c1_ref, w_c1, 4, 0), (c2_ref, w_c2, 2, 1)):
+    for ref, dst, ins, outs in (
+        (c1_ref, w_c1, range(-2, 4), range(-1, 3)),
+        (c1_ref, w_c1b, range(2, 6), range(3, 5)),
+        (c2_ref, w_c2, range(-1, 5), range(0, 4)),
+    ):
         for dy in range(3):
-            for d in (-1, 0, 1):
-                if d == -1:
-                    rows = [[none, none], [ref[dy, 0], none]]
-                elif d == 0:
-                    rows = [[ref[dy, 1], ref[dy, 0]], [ref[dy, 2], ref[dy, 1]]]
-                else:
-                    rows = [[none, ref[dy, 2]], [none, none]]
-                tile = jnp.concatenate([jnp.concatenate(r, axis=1) for r in rows], axis=0)
-                for po in range(outs):
-                    pi = po + shift + d
-                    if 0 <= pi < 4:
-                        dst[
-                            dy * 512 + pi * WIDTH : dy * 512 + (pi + 1) * WIDTH,
-                            po * WIDTH : (po + 1) * WIDTH,
-                        ] = tile
+            for i, c in enumerate(ins):
+                row0 = (dy * len(ins) + i) * CH
+                dst[row0 : row0 + CH, :] = jnp.concatenate(
+                    [ref[dy, c - o + 1] if 0 <= c - o + 1 <= 2 else none for o in outs], axis=1
+                )
 
     def bring(t):
         for d in range(16):
@@ -215,9 +218,7 @@
         pltpu.make_async_copy(src.at[v, pl.ds(me * 16, 16), :], dst.at[v, me], r_sem.at[v]).start()
 
         def one(d):
-            j = d // 2
-            there = (z + 8 + (4 - (j + 1) // 2) * (2 * (j % 2) - 1)) % 8
-            t = (there // 2) * 4 + ((core + d + 1) % 2) * 2 + there % 2
+            t = z_order(d)
             pltpu.make_async_remote_copy(
                 src_ref=src.at[v, pl.ds(t * 16, 16), :], dst_ref=dst.at[v, me],
                 send_sem=s_sem.at[v], recv_sem=r_sem.at[v],
@@ -230,7 +231,7 @@
         pltpu.make_async_copy(src.at[v, pl.ds(xy * 16, 16), :], dst.at[v, xy], r_sem.at[v]).start()
 
         def one(d):
-            t = (xy + d + 1) % 16
+            t = xy_order(d)
             pltpu.make_async_remote_copy(
                 src_ref=src.at[v, pl.ds(t * 16, 16), :], dst_ref=dst.at[v, xy],
                 send_sem=s_sem.at[v], recv_sem=r_sem.at[v],
@@ -270,12 +271,13 @@
     def rows_step(v):
         horizontal(v)
 
-        @pl.when(v == 1)
+        @pl.when(v == 2)
         def _():
             pl.semaphore_wait(barrier, 31)
             start(0)
-
-        @pl.when(v > 0)
+            start(1)
+
+        @pl.when(v > 1)
         def _():
             start(v)
 
@@ -330,17 +332,24 @@
     has_right = jnp.where(block == 31, 0.0, 1.0).astype(F32)
     place = lax.broadcasted_iota(jnp.int32, (GROUP, WIDTH), 0)
 
-    def rims(ref):
-        for p in range(4):
+    lane = lax.broadcasted_iota(jnp.int32, (1, WIDTH), 1)
+    keep_left = jnp.where(lane < CH, has_left, 1.0)
+    keep_right = jnp.where(lane < CH, 1.0, has_right)
+
+    def rims(ref, pairs):
+        for p in range(pairs):
             last = pltpu.roll(ref[p, 8 * GROUP : 9 * GROUP, :].astype(F32), 2, 0)
             ref[p, 0:GROUP, :] = jnp.where(place < 2, 0.0, last).astype(BF16)
             head = pltpu.roll(ref[p, GROUP : 2 * GROUP, :].astype(F32), GROUP - 2, 0)
             ref[p, 9 * GROUP :, :] = jnp.where(place >= GROUP - 2, 0.0, head).astype(BF16)
 
-    def taps(ref):
+    def taps(ref, pairs):
         return jnp.concatenate(
-            [ref[p, dy * GROUP : dy * GROUP + 256, :] for dy in range(3) for p in range(4)], axis=1
+            [ref[p, dy * GROUP : dy * GROUP + 256, :] for dy in range(3) for p in pairs], axis=1
         )
+
+    def leaky(got):
+        return jnp.where(got >= 0, got, 0.1 * got)
 
     def convolve(v):
         for copy in halos(v):
@@ -348,15 +357,14 @@
         here = pad.at[v]
         here[0, inner, :] = (here[0, inner, :].astype(F32) * has_left).astype(BF16)
         here[3, inner, :] = (here[3, inner, :].astype(F32) * has_right).astype(BF16)
-        rims(here)
-        got = jnp.dot(taps(here), w_c1[...], preferred_element_type=F32)
-        got = jnp.where(got >= 0, got, 0.1 * got)
-        hid[0, inner, :] = (got[:, 0:WIDTH] * has_left).astype(BF16)
-        hid[1, inner, :] = got[:, WIDTH : 2 * WIDTH].astype(BF16)
-        hid[2, inner, :] = got[:, 2 * WIDTH : 3 * WIDTH].astype(BF16)
-        hid[3, inner, :] = (got[:, 3 * WIDTH :] * has_right).astype(BF16)
-        rims(hid)
-        got = jnp.dot(taps(hid), w_c2[...], preferred_element_type=F32)
+        rims(here, 4)
+        got = leaky(jnp.dot(taps(here, (0, 1, 2)), w_c1[...], preferred_element_type=F32))
+        hid[0, inner, :] = (got[:, 0:WIDTH] * keep_left).astype(BF16)
+        hid[1, inner, :] = got[:, WIDTH:].astype(BF16)
+        got = leaky(jnp.dot(taps(here, (2, 3)), w_c1b[...], preferred_element_type=F32))
+        hid[2, inner, :] = (got * keep_right).astype(BF16)
+        rims(hid, 3)
+        got = jnp.dot(taps(hid, (0, 1, 2)), w_c2[...], preferred_element_type=F32)
         second = jnp.concatenate([here[1, inner, :], here[2, inner, :]], axis=1)
         result = (second.astype(F32) + got).astype(BF16)
         late = v // 3
@@ -417,8 +425,9 @@
             pltpu.VMEM((2, TOK, WIDTH), F32),
             pltpu.VMEM((2, WIDTH, 6 * WIDTH), BF16),
             pltpu.VMEM((2, WIDTH, 2 * WIDTH), BF16),
-            pltpu.VMEM((1536, 512), BF16),
-            pltpu.VMEM((1536, 256), BF16),
+            pltpu.VMEM((18 * CH, 4 * CH), BF16),
+            pltpu.VMEM((12 * CH, 2 * CH), BF16),
+            pltpu.VMEM((18 * CH, 4 * CH), BF16),
             pltpu.VMEM((2 * WIDTH, WIDTH), BF16),
             pltpu.VMEM((256, 256), BF16),
             pltpu.VMEM((2, 256, 256), BF16),
@@ -431,13 +440,13 @@
             flat4, grid4, flat4, grid4,
             flat4,
             pltpu.VMEM((VL, 4, 10 * GROUP, WIDTH), BF16),
-            pltpu.VMEM((4, 10 * GROUP, WIDTH), BF16),
+            pltpu.VMEM((3, 10 * GROUP, WIDTH), BF16),
             flat4, grid4, flat4, grid4,
             pltpu.SemaphoreType.DMA((7,)),
             sem, sem, sem, sem, sem, sem, sem, sem, sem, sem, sem, sem,
         ],
         compiler_params=pltpu.CompilerParams(
-            collective_id=0, has_side_effects=True, vmem_limit_bytes=48 << 20
+            collective_id=0, has_side_effects=True, vmem_limit_bytes=62 << 20
         ),
     )(x, query_weight, key_weight, value_weight, out_weight.transpose(0, 2, 1), conv_first, conv_second)
     got = got.reshape(VL, 4, 2, 2, XY, 256).transpose(1, 3, 0, 4, 2, 5)

time: 71.9 us -> 67.4 us (0.937)
  local copies, waits for them, and re-layouts: 7.56 us -> 2.71 us
    unnamed x14 -> x0, local copies, waits for them, and re-layouts: 5.89 us -> none
    transpose x1, local copies, waits for them, and re-layouts: 0.54 us -> 1.58 us  [local(): got = got.reshape(VL, 4, 2, 2, XY, 256).transpose(1, 3, 0, 4, 2, 5)]
where the time goes in v2:
time: 67.4 us; the launch traced here: 67.3 us
  Pallas kernels  64.6 us (96%)
  local copies, waits for them, and re-layouts  2.71 us (4%)
    pallas_call x1, Pallas kernels, local(): pl.pallas_call(kernel, out_shape=jax.ShapeDtypeStruct((VL, 16, 16, 256),...  64.6 us
    transpose x1, local copies, waits for them, and re-layouts, local(): got = got.reshape(VL, 4, 2, 2, XY, 256).transpose(1, 3, 0, 4, 2, 5)  1.58 us

profile of v2, /device:TPU:1, one launch (start us, length us, event | category | flops | bytes accessed | tf_op | source)
XLA Modules:
  0.0 67.3 jit_solution(6146071655587453947)
XLA Ops:
  0.0 64.6 %shard_map.73 = bf16[4,16,16,256]{3,2,1,0:T(8,128)(2,1)} custom-call(bf16[8,4,8192]{2,1,0:T(4,128)(2,1)} %bitcast.6, bf16[2,64,128]{2,1,0:T(8,128)(2,1)} %wq_hbm.1, bf16[2,64,128]{2,1,0:T(8,128)(2,1)} %wk_hbm.1, bf16[2,64,128]{2,1,0:T(8,128)(2,1)} %wv_hbm.1, bf16[2,64,128]{2,1,0:T(8,128)(2,1)} %bitcast.7, bf16[3,3,64,64]{3,2,1,0:T(8,128)(2,1)} %c1_hbm.1, ...), custom_call_target="tpu_custom_call" | custom-call | tf_op jit(solution)/shard_map/pallas_call | solution.py:417
  64.6 1.6 %copy.8 = bf16[4,2,4,16,2,256]{5,4,3,2,1,0:T(2,128)(2,1)S(1)} copy(bf16[4,2,4,16,2,256]{5,3,1,4,0,2:T(8,128)(2,1)} %bitcast.5) | data formatting | bytes 1048576 | tf_op jit(solution)/shard_map/transpose | solution.py:452
  66.2 1.1 %reshape.11 = bf16[1,8,4,8192]{3,2,1,0:T(4,128)(2,1)} reshape(bf16[4,2,4,16,2,256]{5,4,3,2,1,0:T(2,128)(2,1)S(1)} %copy.8) | data formatting | bytes 1048576 | tf_op jit(solution)/shard_map/reshape | solution.py:453

commit v3 on v2

--- a/solution.py
+++ b/solution.py
@@ -117,7 +117,7 @@
     ]
     for load in loads:
         load.start()
-    for load in loads:
+    for load in loads[:5]:
         load.wait()
 
     w_qkv[...] = jnp.zeros_like(w_qkv)
@@ -138,6 +138,122 @@
     perm[...] = jnp.where(
         jnp.logical_and(row // 16 == col % 16, row % 16 == col // 16), 1.0, 0.0
     ).astype(BF16)
+    for ln in range(4):
+        va_s[ln, :, WIDTH:] = jnp.ones((TOK, WIDTH), BF16)
+
+    def bring(t):
+        for d in range(16):
+            start = pl.multiple_of(snake(t) * 512 + (d // 2) % 2 * 256, 256)
+            rays = x_in[(d // 4) * 2 + d % 2, :, pl.ds(start, 256)].astype(F32)
+            for p in range(2):
+                x_rows[p, pl.ds(d * 16 + t, VL, stride=256), :] = rays[:, p * WIDTH : (p + 1) * WIDTH]
+
+    fold(16, bring)
+
+    def project_to(i, pair, where):
+        normed = normalise(pair, avg)
+        rows = pair.shape[0]
+        qkv = jnp.dot(normed, w_qkv[i], preferred_element_type=F32).astype(BF16)
+        for h, (ln, start) in enumerate(where):
+            at = pl.ds(start, rows)
+            q_s[ln, at, :] = qkv[:, h * WIDTH : (h + 1) * WIDTH]
+            k_s[ln, at, :] = qkv[:, (2 + h) * WIDTH : (3 + h) * WIDTH]
+            va_s[ln, at, 0:WIDTH] = qkv[:, (4 + h) * WIDTH : (5 + h) * WIDTH]
+
+    def out_project(i, mixed):
+        return lax.dot_general(
+            mixed, w_out[i], (((1,), (1,)), ((), ())), preferred_element_type=F32
+        )
+
+    def horizontal(v):
+        at = pl.ds(pl.multiple_of(v * 256, 256), 256)
+        for p in range(2):
+            project_to(
+                0, x_rows[p, at, :].astype(BF16), [(0, 2 * p * 256), (0, (2 * p + 1) * 256)]
+            )
+        for b in range(4):
+            attend_block(0, slice(b * 256, (b + 1) * 256), q_s, k_s, va_s, m_s)
+        for p in range(2):
+            mixed = jnp.concatenate(
+                [m_s[0, 2 * p * 256 : (2 * p + 1) * 256, :], m_s[0, (2 * p + 1) * 256 : (2 * p + 2) * 256, :]],
+                axis=1,
+            )
+            added = out_project(0, mixed)
+            y_send[v, :, p * WIDTH : (p + 1) * WIDTH] = (x_rows[p, at, :] + added).astype(BF16)
+
+        @pl.when(v % 2 == 1)
+        def _():
+            y_send[v] = jnp.dot(perm[...], y_send[v], preferred_element_type=F32).astype(BF16)
+
+    def send_z(src, dst, v, s_sem, r_sem):
+        pltpu.make_async_copy(src.at[v, pl.ds(me * 16, 16), :], dst.at[v, me], r_sem.at[v]).start()
+
+        def one(d):
+            t = z_order(d)
+            pltpu.make_async_remote_copy(
+                src_ref=src.at[v, pl.ds(t * 16, 16), :], dst_ref=dst.at[v, me],
+                send_sem=s_sem.at[v], recv_sem=r_sem.at[v],
+                device_id=z_peer(t), device_id_type=MESH,
+            ).start()
+
+        fold(15, one)
+
+    def send_xy(src, dst, v, s_sem, r_sem):
+        pltpu.make_async_copy(src.at[v, pl.ds(xy * 16, 16), :], dst.at[v, xy], r_sem.at[v]).start()
+
+        def one(d):
+            t = xy_order(d)
+            pltpu.make_async_remote_copy(
+                src_ref=src.at[v, pl.ds(t * 16, 16), :], dst_ref=dst.at[v, xy],
+                send_sem=s_sem.at[v], recv_sem=r_sem.at[v],
+                device_id=xy_peer(t), device_id_type=MESH,
+            ).start()
+
+        fold(15, one)
+
+    def wait_all(ref, v, sem):
+        pltpu.make_async_copy(ref.at[v], ref.at[v], sem.at[v]).wait()
+
+    def wait_sent(ref, v, sem):
+        part = ref.at[v, pl.ds(0, 15)]
+        pltpu.make_async_copy(part, part, sem.at[v]).wait()
+
+    def reorder(src, dst, v):
+        rows = jnp.concatenate([src[v, s] for s in range(16)], axis=0)
+        dst[v] = jnp.dot(perm[...], rows, preferred_element_type=F32).astype(BF16)
+
+    def first_stage(along_z, src, dst, v, s_sem, r_sem):
+        @pl.when(along_z)
+        def _():
+            send_z(src, dst, v, s_sem, r_sem)
+
+        @pl.when(jnp.logical_not(along_z))
+        def _():
+            send_xy(src, dst, v, s_sem, r_sem)
+
+    def start(v):
+        first_stage(v % 2 == 0, y_send, a_recv, v, s_a, r_a)
+
+    def forward(v):
+        wait_all(a_recv, v, r_a)
+        reorder(a_recv, b_send, v)
+        first_stage(v % 2 == 1, b_send, r_recv, v, s_b, r_b)
+
+    def rows_step(v):
+        horizontal(v)
+
+        @pl.when(v == 1)
+        def _():
+            pl.semaphore_wait(barrier, 31)
+            start(0)
+
+        @pl.when(v > 0)
+        def _():
+            start(v)
+
+    fold(VL, rows_step)
+    for load in loads[5:]:
+        load.wait()
     for ref, a, b in ((perm_in, row, col), (perm_out, col, row)):
         for odd in range(2):
             if odd:
@@ -154,9 +270,6 @@
         else:
             here = jnp.logical_and(col // 16 == chip, col % 16 == row // 16)
         perm_end[odd] = jnp.where(here, 1.0, 0.0).astype(BF16)
-    for ln in range(4):
-        va_s[ln, :, WIDTH:] = jnp.ones((TOK, WIDTH), BF16)
-
     none = jnp.zeros((CH, CH), BF16)
     for ref, dst, ins, outs in (
         (c1_ref, w_c1, range(-2, 4), range(-1, 3)),
@@ -170,118 +283,6 @@
                     [ref[dy, c - o + 1] if 0 <= c - o + 1 <= 2 else none for o in outs], axis=1
                 )
 
-    def bring(t):
-        for d in range(16):
-            start = pl.multiple_of(snake(t) * 512 + (d // 2) % 2 * 256, 256)
-            rays = x_in[(d // 4) * 2 + d % 2, :, pl.ds(start, 256)].astype(F32)
-            for p in range(2):
-                x_rows[p, pl.ds(d * 16 + t, VL, stride=256), :] = rays[:, p * WIDTH : (p + 1) * WIDTH]
-
-    fold(16, bring)
-
-    def project_to(i, pair, where):
-        normed = normalise(pair, avg)
-        rows = pair.shape[0]
-        qkv = jnp.dot(normed, w_qkv[i], preferred_element_type=F32).astype(BF16)
-        for h, (ln, start) in enumerate(where):
-            at = pl.ds(start, rows)
-            q_s[ln, at, :] = qkv[:, h * WIDTH : (h + 1) * WIDTH]
-            k_s[ln, at, :] = qkv[:, (2 + h) * WIDTH : (3 + h) * WIDTH]
-            va_s[ln, at, 0:WIDTH] = qkv[:, (4 + h) * WIDTH : (5 + h) * WIDTH]
-
-    def out_project(i, mixed):
-        return lax.dot_general(
-            mixed, w_out[i], (((1,), (1,)), ((), ())), preferred_element_type=F32
-        )
-
-    def horizontal(v):
-        at = pl.ds(pl.multiple_of(v * 256, 256), 256)
-        for p in range(2):
-            project_to(
-                0, x_rows[p, at, :].astype(BF16), [(0, 2 * p * 256), (0, (2 * p + 1) * 256)]
-            )
-        for b in range(4):
-            attend_block(0, slice(b * 256, (b + 1) * 256), q_s, k_s, va_s, m_s)
-        for p in range(2):
-            mixed = jnp.concatenate(
-                [m_s[0, 2 * p * 256 : (2 * p + 1) * 256, :], m_s[0, (2 * p + 1) * 256 : (2 * p + 2) * 256, :]],
-                axis=1,
-            )
-            added = out_project(0, mixed)
-            y_send[v, :, p * WIDTH : (p + 1) * WIDTH] = (x_rows[p, at, :] + added).astype(BF16)
-
-        @pl.when(v % 2 == 1)
-        def _():
-            y_send[v] = jnp.dot(perm[...], y_send[v], preferred_element_type=F32).astype(BF16)
-
-    def send_z(src, dst, v, s_sem, r_sem):
-        pltpu.make_async_copy(src.at[v, pl.ds(me * 16, 16), :], dst.at[v, me], r_sem.at[v]).start()
-
-        def one(d):
-            t = z_order(d)
-            pltpu.make_async_remote_copy(
-                src_ref=src.at[v, pl.ds(t * 16, 16), :], dst_ref=dst.at[v, me],
-                send_sem=s_sem.at[v], recv_sem=r_sem.at[v],
-                device_id=z_peer(t), device_id_type=MESH,
-            ).start()
-
-        fold(15, one)
-
-    def send_xy(src, dst, v, s_sem, r_sem):
-        pltpu.make_async_copy(src.at[v, pl.ds(xy * 16, 16), :], dst.at[v, xy], r_sem.at[v]).start()
-
-        def one(d):
-            t = xy_order(d)
-            pltpu.make_async_remote_copy(
-                src_ref=src.at[v, pl.ds(t * 16, 16), :], dst_ref=dst.at[v, xy],
-                send_sem=s_sem.at[v], recv_sem=r_sem.at[v],
-                device_id=xy_peer(t), device_id_type=MESH,
-            ).start()
-
-        fold(15, one)
-
-    def wait_all(ref, v, sem):
-        pltpu.make_async_copy(ref.at[v], ref.at[v], sem.at[v]).wait()
-
-    def wait_sent(ref, v, sem):
-        part = ref.at[v, pl.ds(0, 15)]
-        pltpu.make_async_copy(part, part, sem.at[v]).wait()
-
-    def reorder(src, dst, v):
-        rows = jnp.concatenate([src[v, s] for s in range(16)], axis=0)
-        dst[v] = jnp.dot(perm[...], rows, preferred_element_type=F32).astype(BF16)
-
-    def first_stage(along_z, src, dst, v, s_sem, r_sem):
-        @pl.when(along_z)
-        def _():
-            send_z(src, dst, v, s_sem, r_sem)
-
-        @pl.when(jnp.logical_not(along_z))
-        def _():
-            send_xy(src, dst, v, s_sem, r_sem)
-
-    def start(v):
-        first_stage(v % 2 == 0, y_send, a_recv, v, s_a, r_a)
-
-    def forward(v):
-        wait_all(a_recv, v, r_a)
-        reorder(a_recv, b_send, v)
-        first_stage(v % 2 == 1, b_send, r_recv, v, s_b, r_b)
-
-    def rows_step(v):
-        horizontal(v)
-
-        @pl.when(v == 2)
-        def _():
-            pl.semaphore_wait(barrier, 31)
-            start(0)
-            start(1)
-
-        @pl.when(v > 1)
-        def _():
-            start(v)
-
-    fold(VL, rows_step)
     fold(VL, lambda i: forward(i + 1 - 2 * (i % 2)))
 
     def columns(v):
@@ -408,6 +409,9 @@
 
 def local(light_field, query_weight, key_weight, value_weight, out_weight, conv_first, conv_second):
     x = light_field.reshape(8, VL, 8192)
+    operands = (
+        x, query_weight, key_weight, value_weight, out_weight.transpose(0, 2, 1), conv_first, conv_second
+    )
     vmem = pl.BlockSpec(memory_space=pltpu.VMEM)
     grid4 = pltpu.VMEM((VL, 16, 16, 256), BF16)
     flat4 = pltpu.VMEM((VL, 256, 256), BF16)
@@ -446,9 +450,9 @@
             sem, sem, sem, sem, sem, sem, sem, sem, sem, sem, sem, sem,
         ],
         compiler_params=pltpu.CompilerParams(
-            collective_id=0, has_side_effects=True, vmem_limit_bytes=62 << 20
+            collective_id=0, has_side_effects=True, vmem_limit_bytes=48 << 20
         ),
-    )(x, query_weight, key_weight, value_weight, out_weight.transpose(0, 2, 1), conv_first, conv_second)
+    )(*[pltpu.with_memory_space_constraint(a, pltpu.MemorySpace.HBM) for a in operands])
     got = got.reshape(VL, 4, 2, 2, XY, 256).transpose(1, 3, 0, 4, 2, 5)
     return got.reshape(1, 8, VL, 8192)
 

time: 67.4 us -> 64.9 us (0.963)
  Pallas kernels: 64.6 us -> 63.1 us
  local copies, waits for them, and re-layouts: 2.71 us -> 1.67 us
    pallas_call x1, Pallas kernels: 64.6 us -> 63.1 us  [local(): pl.pallas_call(kernel, out_shape=jax.ShapeDtypeStruct((VL, 16, 16, 256),...]
    transpose x1, local copies, waits for them, and re-layouts: 1.58 us -> 0.54 us  [local(): got = got.reshape(VL, 4, 2, 2, XY, 256).transpose(1, 3, 0, 4, 2, 5)]
where the time goes in v3:
time: 64.9 us; the launch traced here: 64.8 us
  Pallas kernels  63.1 us (97%)
  local copies, waits for them, and re-layouts  1.67 us (3%)
    pallas_call x1, Pallas kernels, local(): pl.pallas_call(kernel, out_shape=jax.ShapeDtypeStruct((VL, 16, 16, 256),...  63.1 us

profile of v3, /device:TPU:1, one launch (start us, length us, event | category | flops | bytes accessed | tf_op | source)
XLA Modules:
  0.0 64.8 jit_solution(14403668497807146358)
XLA Ops:
  0.0 63.1 %shard_map.73 = bf16[4,16,16,256]{3,2,1,0:T(8,128)(2,1)S(1)} custom-call(bf16[8,4,8192]{2,1,0:T(4,128)(2,1)} %bitcast.6, bf16[2,64,128]{2,1,0:T(8,128)(2,1)} %wq_hbm.1, bf16[2,64,128]{2,1,0:T(8,128)(2,1)} %wk_hbm.1, bf16[2,64,128]{2,1,0:T(8,128)(2,1)} %wv_hbm.1, bf16[2,64,128]{2,1,0:T(8,128)(2,1)} %bitcast.7, bf16[3,3,64,64]{3,2,1,0:T(8,128)(2,1)} %c1_hbm.1, ...), custom_call_target="tpu_custom_call" | custom-call | tf_op jit(solution)/shard_map/pallas_call | solution.py:421
  63.1 0.5 copy.8
  63.7 1.1 %reshape.11 = bf16[1,8,4,8192]{3,2,1,0:T(4,128)(2,1)} reshape(bf16[4,2,4,16,2,256]{5,4,3,2,1,0:T(2,128)(2,1)S(1)} %copy.8) | data formatting | bytes 1048576 | tf_op jit(solution)/shard_map/reshape | solution.py:457

commit v4 on v3

--- a/solution.py
+++ b/solution.py
@@ -283,7 +283,7 @@
                     [ref[dy, c - o + 1] if 0 <= c - o + 1 <= 2 else none for o in outs], axis=1
                 )
 
-    fold(VL, lambda i: forward(i + 1 - 2 * (i % 2)))
+    fold(VL, lambda i: forward(i + (1 - 2 * i) * (1 - i // 2)))
 
     def columns(v):
         wait_all(r_recv, v, r_b)
@@ -303,6 +303,9 @@
         at = pl.ds(pl.multiple_of(v * 256, 256), 256)
         for ln in range(4):
             attend_block(ln, at, q_s, k_s, va_s, m_s)
+
+    def join(v):
+        at = pl.ds(pl.multiple_of(v * 256, 256), 256)
         for p in range(2):
             mixed = jnp.concatenate([m_s[2 * p, at, :], m_s[2 * p + 1, at, :]], axis=1)
             added = out_project(1, mixed)
@@ -352,9 +355,11 @@
     def leaky(got):
         return jnp.where(got >= 0, got, 0.1 * got)
 
-    def convolve(v):
+    def meet(v):
         for copy in halos(v):
             copy.wait()
+
+    def convolve(v):
         here = pad.at[v]
         here[0, inner, :] = (here[0, inner, :].astype(F32) * has_left).astype(BF16)
         here[3, inner, :] = (here[3, inner, :].astype(F32) * has_right).astype(BF16)
@@ -370,6 +375,8 @@
         result = (second.astype(F32) + got).astype(BF16)
         late = v // 3
         b2_send[v] = jnp.dot(perm_out[1 - late], result, preferred_element_type=F32).astype(BF16)
+
+    def leave(v):
         first_stage(v < 3, b2_send, a2_recv, v, s_b2, r_b2)
 
     def back(v):
@@ -377,16 +384,27 @@
         reorder(a2_recv, y2_send, v)
         first_stage(v == 3, y2_send, f_recv, v, s_a2, r_a2)
 
+    def columns_start(v):
+        attend(v)
+        join(v)
+
+    fold(2, columns_start)
+
     def columns_step(i):
-        @pl.when(i < VL)
-        def _():
-            attend(i)
-
-        @pl.when(i > 0)
-        def _():
-            convolve(i - 1)
-
-    fold(VL + 1, columns_step)
+        meet(i)
+        attend(i + 2)
+        convolve(i)
+        join(i + 2)
+        leave(i)
+
+    fold(2, columns_step)
+
+    def columns_end(i):
+        meet(i + 2)
+        convolve(i + 2)
+        leave(i + 2)
+
+    fold(2, columns_end)
     fold(VL, lambda i: back(i + i // 2 - 3 * (i // 3) + i // 3))
 
     def arrive(v):

time: 64.9 us -> 63.2 us (0.974)
  Pallas kernels: 63.1 us -> 61.4 us
    pallas_call x1, Pallas kernels: 63.1 us -> 61.4 us  [local(): pl.pallas_call(kernel, out_shape=jax.ShapeDtypeStruct((VL, 16, 16, 256),...]
where the time goes in v4:
time: 63.2 us; the launch traced here: 63.1 us
  Pallas kernels  61.4 us (97%)
  local copies, waits for them, and re-layouts  1.67 us (3%)
    pallas_call x1, Pallas kernels, local(): pl.pallas_call(kernel, out_shape=jax.ShapeDtypeStruct((VL, 16, 16, 256),...  61.4 us

profile of v4, /device:TPU:1, one launch (start us, length us, event | category | flops | bytes accessed | tf_op | source)
XLA Modules:
  0.0 63.1 jit_solution(4217206078302420330)
XLA Ops:
  0.0 61.4 %shard_map.73 = bf16[4,16,16,256]{3,2,1,0:T(8,128)(2,1)S(1)} custom-call(bf16[8,4,8192]{2,1,0:T(4,128)(2,1)} %bitcast.6, bf16[2,64,128]{2,1,0:T(8,128)(2,1)} %wq_hbm.1, bf16[2,64,128]{2,1,0:T(8,128)(2,1)} %wk_hbm.1, bf16[2,64,128]{2,1,0:T(8,128)(2,1)} %wv_hbm.1, bf16[2,64,128]{2,1,0:T(8,128)(2,1)} %bitcast.7, bf16[3,3,64,64]{3,2,1,0:T(8,128)(2,1)} %c1_hbm.1, ...), custom_call_target="tpu_custom_call" | custom-call | tf_op jit(solution)/shard_map/pallas_call | solution.py:439
  61.4 0.5 copy.8
  61.9 1.1 %reshape.11 = bf16[1,8,4,8192]{3,2,1,0:T(4,128)(2,1)} reshape(bf16[4,2,4,16,2,256]{5,4,3,2,1,0:T(2,128)(2,1)S(1)} %copy.8) | data formatting | bytes 1048576 | tf_op jit(solution)/shard_map/reshape | solution.py:475

commit v5 on v4

--- a/solution.py
+++ b/solution.py
@@ -263,12 +263,13 @@
                 here = jnp.logical_and(a // 32 == (b // 2) % 8, (a // 2) % 16 == b // 16)
                 here = jnp.logical_and(here, a % 2 == b % 2)
             ref[odd] = jnp.where(here, 1.0, 0.0).astype(BF16)
-    chip = snake(row % 16)
+    chip = snake((row // 2) % 16)
+    device = row // 64 * 4 + row % 2 * 2 + (row // 32) % 2
     for odd in range(2):
         if odd:
-            here = jnp.logical_and(col % 16 == chip, col // 16 == row // 16)
+            here = jnp.logical_and(col % 16 == chip, col // 16 == device)
         else:
-            here = jnp.logical_and(col // 16 == chip, col % 16 == row // 16)
+            here = jnp.logical_and(col // 16 == chip, col % 16 == device)
         perm_end[odd] = jnp.where(here, 1.0, 0.0).astype(BF16)
     none = jnp.zeros((CH, CH), BF16)
     for ref, dst, ins, outs in (
@@ -411,8 +412,8 @@
         wait_all(f_recv, v, r_a2)
         rows = jnp.concatenate([f_recv[v, s] for s in range(16)], axis=0)
         got = jnp.dot(perm_end[v // 3], rows, preferred_element_type=F32).astype(BF16)
-        for s in range(16):
-            out_ref[v, s] = got[s * 16 : (s + 1) * 16, :]
+        for u in range(8):
+            out_ref[u, v] = got[u * 32 : (u + 1) * 32, :]
 
     fold(VL, arrive)
 
@@ -438,7 +439,7 @@
     taps = pltpu.VMEM((3, 3, CH, CH), BF16)
     got = pl.pallas_call(
         kernel,
-        out_shape=jax.ShapeDtypeStruct((VL, 16, 16, 256), BF16),
+        out_shape=jax.ShapeDtypeStruct((8, VL, 32, 256), BF16),
         in_specs=[pl.BlockSpec(memory_space=pltpu.MemorySpace.HBM)] * 7,
         out_specs=vmem,
         scratch_shapes=[
@@ -471,7 +472,6 @@
             collective_id=0, has_side_effects=True, vmem_limit_bytes=48 << 20
         ),
     )(*[pltpu.with_memory_space_constraint(a, pltpu.MemorySpace.HBM) for a in operands])
-    got = got.reshape(VL, 4, 2, 2, XY, 256).transpose(1, 3, 0, 4, 2, 5)
     return got.reshape(1, 8, VL, 8192)
 
 

time: 63.2 us -> 63.1 us (level)
  no operation moved by 1% of the time
where the time goes in v5:
time: 63.1 us; the launch traced here: 63 us
  Pallas kernels  61.8 us (98%)
  local copies, waits for them, and re-layouts  1.17 us (2%)
    pallas_call x1, Pallas kernels, local(): pl.pallas_call(kernel, out_shape=jax.ShapeDtypeStruct((8, VL, 32, 256), B...  61.8 us

profile of v5, /device:TPU:1, one launch (start us, length us, event | category | flops | bytes accessed | tf_op | source)
XLA Modules:
  0.0 63.0 jit_solution(6552395443983203329)
XLA Ops:
  0.0 61.8 %shard_map.73 = bf16[8,4,32,256]{3,2,1,0:T(8,128)(2,1)S(1)} custom-call(bf16[8,4,8192]{2,1,0:T(4,128)(2,1)} %bitcast.4, bf16[2,64,128]{2,1,0:T(8,128)(2,1)} %wq_hbm.1, bf16[2,64,128]{2,1,0:T(8,128)(2,1)} %wk_hbm.1, bf16[2,64,128]{2,1,0:T(8,128)(2,1)} %wv_hbm.1, bf16[2,64,128]{2,1,0:T(8,128)(2,1)} %bitcast.5, bf16[3,3,64,64]{3,2,1,0:T(8,128)(2,1)} %c1_hbm.1, ...), custom_call_target="tpu_custom_call" | custom-call | tf_op jit(solution)/shard_map/pallas_call | solution.py:440
  61.8 1.2 %reshape.7 = bf16[1,8,4,8192]{3,2,1,0:T(4,128)(2,1)} reshape(bf16[8,4,32,256]{3,2,1,0:T(8,128)(2,1)S(1)} %shard_map.73) | data formatting | bytes 1048576 | tf_op jit(solution)/shard_map/reshape | solution.py:475
